TPU v7x, 256 devices: a whole 4x4x8 slice. The times are simulated.
256 devices in a mesh: tm: 64 (over y, z, core), chan: 4 (over x).
Axes of the slice: x: 4, y: 4, z: 8, core: 2. Of those that a mesh axis runs over, the one named last changes fastest.
Arguments:
- signals: bfloat16 [262144, 2048], P('tm', 'chan')
- channel_node: int32 [2048], P('chan'), may hold values from 0 to 127, as said below
- lag_offsets: int32 [8], replicated, may hold values from 0 to 512, as said below
Outputs:
- r_factor: float32 [1024, 1024], replicated
Inputs may be any that keep to these rules, and one draw needn't show every extreme that they name: `channel_node`: every node is named by exactly 16 channels; which channels, and so which channel groups, is drawn. `lag_offsets`: strictly increasing; the first is 0 and the last is 512.
All inputs are finite; a program needn't handle non-finite values.
Results may differ from a plain program's by a relative error of at most 0.0003.
Values sent between devices are 32-bit elements; how exact they have to be, the bound alone decides.
A program may use at most 64 MiB of HBM per device.

v0:
```python
import math
import jax
import jax.numpy as jnp
from jax import lax
from jax.sharding import PartitionSpec as P

NODES = 128
CH = 2048
MAXLAG = 512


def from_behind(value, axis, steps):
    count = lax.axis_size(axis)
    leading, last = (max(0, -steps), min(count, count - steps))
    return lax.ppermute(value, axis, [(source, source + steps) for source in range(leading, last)])


def on_device(signals, channel_node, lag_offsets):
    group_count = lax.axis_size("chan")
    lag_count = lag_offsets.shape[0]
    group_width = NODES // group_count
    onehot = (channel_node[:, None] == jnp.arange(NODES, dtype=jnp.int32)[None, :]).astype(
        jnp.bfloat16
    )
    partial_value = jnp.dot(signals, onehot, preferred_element_type=jnp.float32)
    node_scale = 1.0 / math.sqrt(CH // NODES)
    node_share = (
        lax.psum_scatter(partial_value, "chan", scatter_dimension=1, tiled=True) * node_scale
    )
    rim_rows = from_behind(node_share[:MAXLAG], "tm", -1)
    extended = jnp.concatenate([node_share, rim_rows], axis=0)
    time_rows = node_share.shape[0]
    columns = []
    for lag_index in range(lag_count):
        columns.append(
            lax.dynamic_slice(
                extended, (lag_offsets[lag_index], jnp.int32(0)), (time_rows, group_width)
            )
        )
    panel = jnp.concatenate(columns, axis=1)
    hankel = lax.all_to_all(panel, "chan", split_axis=0, concat_axis=1, tiled=True)
    row_total = hankel.shape[0] * lax.axis_size("tm") * group_count
    local_gram = lax.dot_general(
        hankel,
        hankel,
        (((0,), (0,)), ((), ())),
        precision=lax.Precision.HIGHEST,
        preferred_element_type=jnp.float32,
    )
    gram_matrix = lax.psum(local_gram, ("tm", "chan"))
    return jnp.linalg.cholesky(gram_matrix / row_total).T


def solution(mesh):
    in_specs = (P("tm", "chan"), P("chan"), P())
    out_specs = P()
    return jax.shard_map(
        on_device, mesh=mesh, in_specs=in_specs, out_specs=out_specs, check_vma=False
    )
```

profile of v0, /device:TPU:2, one launch (start us, length us, event | category | flops | bytes accessed | tf_op | source)
XLA Modules:
  0.0 642.1 jit_solution(7835683541833374549)
XLA Ops:
  6.5 5.2 convolution_bitcast_fusion
  11.8 34.0 %reduce-scatter.2.cloned.1.call-done = f32[4096,32]{0,1:T(8,128)} async-done(((f32[4096,128]{0,1:T(8,128)}), f32[4096,32]{0,1:T(8,128)}) %reduce-scatter.2.cloned.1.call-update) | async-done | bytes 524304 | tf_op jit(solution)/shard_map/reduce_scatter | solution.py:28
  67.2 53.2 %all_to_all.19 = f32[4,1024,256]{1,2,0:T(8,128)S(1)} all-to-all(f32[4,1024,256]{1,2,0:T(8,128)S(1)} %bitcast.64), channel_id=1, replica_groups=mesh['tm'=64,'chan'=4] {'chan'}, dimensions={0} | all-to-all | bytes 8388608 | tf_op jit(solution)/shard_map/all_to_all | solution.py:41
  120.4 14.9 %fusion.48 = f32[1024,1024]{0,1:T(8,128)} fusion(f32[1024,1024]{0,1:T(8,128)S(1)} %bitcast.66), kind=kOutput, calls=%fused_computation.117 | convolution fusion | flops 12884901888 | bytes 8388608 | tf_op jit(solution)/shard_map/dot_general | solution.py:43
  135.3 269.4 %all-reduce.3.cloned.1.call-done = f32[1024,1024]{0,1:T(8,128)} async-done(((f32[1024,1024]{0,1:T(8,128)}), f32[1024,1024]{0,1:T(8,128)}) %all-reduce.3.cloned.1.call-update) | async-done | bytes 4194320 | tf_op jit(solution)/shard_map/psum | solution.py:50
  404.7 5.0 broadcast_multiply_fusion
  409.7 5.8 copy.9
  415.6 4.4 fusion
  422.0 11.7 %cholesky.223 = f32[128,128]{1,0:T(8,128)S(1)} custom-call(f32[128,128]{1,0:T(8,128)S(1)} %cholesky.580), custom_call_target="Cholesky" | custom-call | tf_op jit(solution)/shard_map/jit(cholesky)/cholesky | solution.py:51
  433.7 9.8 %custom-call.59 = f32[1,128,128]{1,2,0:T(8,128)S(1)} custom-call(f32[1,128,128]{2,1,0:T(8,128)S(1)} %get-tuple-element.26), custom_call_target="InvertDiagBlocksLowerTriangular" | custom-call | tf_op jit(solution)/shard_map/jit(cholesky)/cholesky | solution.py:51
  443.6 2.5 cholesky.255
  446.1 2.3 constant_dynamic-update-slice_fusion
  450.0 11.9 %cholesky.244 = f32[128,128]{1,0:T(8,128)S(1)} custom-call(f32[128,128]{1,0:T(8,128)S(1)} %cholesky.584), custom_call_target="Cholesky" | custom-call | tf_op jit(solution)/shard_map/jit(cholesky)/cholesky | solution.py:51
  462.5 9.8 %custom-call.60 = f32[1,128,128]{1,2,0:T(8,128)S(1)} custom-call(f32[1,128,128]{2,1,0:T(8,128)S(1)} %get-tuple-element.23), custom_call_target="InvertDiagBlocksLowerTriangular" | custom-call | tf_op jit(solution)/shard_map/jit(cholesky)/cholesky | solution.py:51
  473.5 2.1 convolution_subtract_fusion.1
  475.6 11.7 %cholesky.468 = f32[128,128]{1,0:T(8,128)S(1)} custom-call(f32[128,128]{1,0:T(8,128)S(1)} %cholesky.589), custom_call_target="Cholesky" | custom-call | tf_op jit(solution)/shard_map/jit(cholesky)/cholesky | solution.py:51
  488.6 9.8 %custom-call.61 = f32[1,128,128]{1,2,0:T(8,128)S(1)} custom-call(f32[1,128,128]{2,1,0:T(8,128)S(1)} %get-tuple-element.20), custom_call_target="InvertDiagBlocksLowerTriangular" | custom-call | tf_op jit(solution)/shard_map/jit(cholesky)/cholesky | solution.py:51
  499.6 2.3 convolution_subtract_fusion.2
  501.9 11.9 %cholesky.487 = f32[128,128]{1,0:T(8,128)S(1)} custom-call(f32[128,128]{1,0:T(8,128)S(1)} %cholesky.594), custom_call_target="Cholesky" | custom-call | tf_op jit(solution)/shard_map/jit(cholesky)/cholesky | solution.py:51
  515.1 9.8 %custom-call.62 = f32[1,128,128]{1,2,0:T(8,128)S(1)} custom-call(f32[1,128,128]{2,1,0:T(8,128)S(1)} %get-tuple-element.17), custom_call_target="InvertDiagBlocksLowerTriangular" | custom-call | tf_op jit(solution)/shard_map/jit(cholesky)/cholesky | solution.py:51
  526.0 2.4 convolution_subtract_fusion.3
  528.4 11.7 %cholesky.506 = f32[128,128]{1,0:T(8,128)S(1)} custom-call(f32[128,128]{1,0:T(8,128)S(1)} %cholesky.599), custom_call_target="Cholesky" | custom-call | tf_op jit(solution)/shard_map/jit(cholesky)/cholesky | solution.py:51
  541.5 10.2 %custom-call.63 = f32[1,128,128]{1,2,0:T(8,128)S(1)} custom-call(f32[1,128,128]{2,1,0:T(8,128)S(1)} %get-tuple-element.14), custom_call_target="InvertDiagBlocksLowerTriangular" | custom-call | tf_op jit(solution)/shard_map/jit(cholesky)/cholesky | solution.py:51
  552.7 2.3 convolution_subtract_fusion.4
  555.0 11.7 %cholesky.526 = f32[128,128]{1,0:T(8,128)S(1)} custom-call(f32[128,128]{1,0:T(8,128)S(1)} %cholesky.604), custom_call_target="Cholesky" | custom-call | tf_op jit(solution)/shard_map/jit(cholesky)/cholesky | solution.py:51
  568.0 9.8 %custom-call.64 = f32[1,128,128]{1,2,0:T(8,128)S(1)} custom-call(f32[1,128,128]{2,1,0:T(8,128)S(1)} %get-tuple-element.11), custom_call_target="InvertDiagBlocksLowerTriangular" | custom-call | tf_op jit(solution)/shard_map/jit(cholesky)/cholesky | solution.py:51
  578.7 2.0 convolution_subtract_fusion.5
  580.7 11.9 %cholesky.546 = f32[128,128]{1,0:T(8,128)S(1)} custom-call(f32[128,128]{1,0:T(8,128)S(1)} %cholesky.609), custom_call_target="Cholesky" | custom-call | tf_op jit(solution)/shard_map/jit(cholesky)/cholesky | solution.py:51
  593.9 9.8 %custom-call.65 = f32[1,128,128]{1,2,0:T(8,128)S(1)} custom-call(f32[1,128,128]{2,1,0:T(8,128)S(1)} %get-tuple-element.8), custom_call_target="InvertDiagBlocksLowerTriangular" | custom-call | tf_op jit(solution)/shard_map/jit(cholesky)/cholesky | solution.py:51
  606.3 11.7 %cholesky.564 = f32[128,128]{1,0:T(8,128)S(1)} custom-call(f32[128,128]{1,0:T(8,128)S(1)} %convolution_subtract_fusion.6), custom_call_target="Cholesky" | custom-call | tf_op jit(solution)/shard_map/jit(cholesky)/cholesky | solution.py:51
  625.0 4.8 select_bitcast_fusion
  629.7 5.3 copy.10
  (52 shorter events, 27.1 us)
Async XLA Ops:
  6.5 41.7 %copy-start.1 = (s32[8]{0:T(128)S(1)}, s32[8]{0:T(128)}, u32[]{:S(2)}) copy-start(s32[8]{0:T(128)} %param.5) | copy-start | bytes 100
  6.5 39.3 %reduce-scatter.2.cloned.1.call-start = ((), (), s32[]{:S(2)}) async-start(), calls=%async_computation.2 | async-start | bytes 2621440 | tf_op jit(solution)/shard_map/reduce_scatter | solution.py:28
  11.7 393.0 %all-reduce.3.cloned.1.call-start = ((), (), s32[]{:S(2)}) async-start(), calls=%async_computation.3 | async-start | bytes 8388608 | tf_op jit(solution)/shard_map/psum | solution.py:50
  46.9 16.8 %collective-permute-start = (f32[512,32]{0,1:T(8,128)S(1)}, f32[512,32]{0,1:T(8,128)S(1)}, u32[]{:S(2)}, u32[]{:S(2)}) collective-permute-start(f32[512,32]{0,1:T(8,128)S(1)} %slice.213), channel_id=1, source_target_pairs={{4,0},{8,4},{12,8},{16,12},{20,16},{24,20},{28,24},{32,28},{36,32}... | collective-permute-start | bytes 196616 | tf_op jit(solution)/shard_map/ppermute | solution.py:15
  420.1 1.9 copy-start
Sparse Core Ops, SparseCore 0:
  11.9 33.9 reduce-scatter.1
  135.4 269.2 all-reduce.2
where the time goes:
time: 647 us; the launch traced here: 642 us
  waiting for transfers between devices  303 us (47%)
  other arithmetic  190 us (29%)
  blocking collectives  53.2 us (8%)
  matrix products  43 us (7%)
  between operations  33.6 us (5%)
  local copies, waits for them, and re-layouts  16.9 us (3%)
    psum x1, waiting for transfers between devices, on_device(): gram_matrix = lax.psum(local_gram, ('tm', 'chan'))  269 us
    another operation x30, other arithmetic, on_device(): return jnp.linalg.cholesky(gram_matrix / row_total).T  172 us
    all_to_all x1, blocking collectives, on_device(): lax.all_to_all(panel, 'chan', split_axis=0, concat_axis=1, tiled=True)  53.2 us
    reduce_scatter x1, waiting for transfers between devices, on_device(): lax.psum_scatter(partial_value, 'chan', scatter_dimension=1, tiled=True)  34 us
    another operation x14, matrix products, on_device(): return jnp.linalg.cholesky(gram_matrix / row_total).T  22.9 us
    dot_general x1, matrix products, on_device(): lax.dot_general(hankel, hankel, (((0,), (0,)), ((), ())), precision=lax.P...  14.9 us
  transfers between devices with their start and end apart: 3, of which 2 were waited for; matrix products, arithmetic and copies ran while one was open for 0% of the time, Pallas kernels for 0%

commit v1 on v0

--- a/solution.py
+++ b/solution.py
@@ -47,7 +47,9 @@
         precision=lax.Precision.HIGHEST,
         preferred_element_type=jnp.float32,
     )
-    gram_matrix = lax.psum(local_gram, ("tm", "chan"))
+    gram_matrix = local_gram
+    for kk in ("chan", "tm"):
+        gram_matrix = lax.psum(gram_matrix, kk)
     return jnp.linalg.cholesky(gram_matrix / row_total).T
 
 

time: 647 us -> 675 us (1.043)
  waiting for transfers between devices: 303 us -> 332 us
    psum x1 -> x2, waiting for transfers between devices: 269 us -> 298 us  [on_device(): gram_matrix = lax.psum(gram_matrix, kk)]
  transfers between devices with their start and end apart: 3 -> 4, of which waited for: 2 -> 3; matrix products, arithmetic and copies ran while one was open for 0% -> 0% of each run, Pallas kernels for 0% -> 0%
where the time goes in v1:
time: 675 us; the launch traced here: 670 us
  waiting for transfers between devices  332 us (49%)
  other arithmetic  190 us (28%)
  blocking collectives  53.2 us (8%)
  matrix products  43 us (6%)
  between operations  33.3 us (5%)
  local copies, waits for them, and re-layouts  16.9 us (3%)
    psum x2, waiting for transfers between devices, on_device(): gram_matrix = lax.psum(gram_matrix, kk)  298 us
    another operation x30, other arithmetic, on_device(): return jnp.linalg.cholesky(gram_matrix / row_total).T  172 us
    all_to_all x1, blocking collectives, on_device(): lax.all_to_all(panel, 'chan', split_axis=0, concat_axis=1, tiled=True)  53.2 us
    reduce_scatter x1, waiting for transfers between devices, on_device(): lax.psum_scatter(partial_value, 'chan', scatter_dimension=1, tiled=True)  34 us
    another operation x14, matrix products, on_device(): return jnp.linalg.cholesky(gram_matrix / row_total).T  22.9 us
    dot_general x1, matrix products, on_device(): lax.dot_general(hankel, hankel, (((0,), (0,)), ((), ())), precision=lax.P...  14.9 us
  transfers between devices with their start and end apart: 4, of which 3 were waited for; matrix products, arithmetic and copies ran while one was open for 0% of the time, Pallas kernels for 0%

profile of v1, /device:TPU:2, one launch (start us, length us, event | category | flops | bytes accessed | tf_op | source)
XLA Modules:
  0.0 670.3 jit_solution(10515232850206423874)
XLA Ops:
  6.5 5.2 convolution_bitcast_fusion
  11.8 34.0 %reduce-scatter.2.cloned.1.call-done = f32[4096,32]{0,1:T(8,128)} async-done(((f32[4096,128]{0,1:T(8,128)}), f32[4096,32]{0,1:T(8,128)}) %reduce-scatter.2.cloned.1.call-update) | async-done | bytes 524304 | tf_op jit(solution)/shard_map/reduce_scatter | solution.py:28
  67.2 53.2 %all_to_all.19 = f32[4,1024,256]{1,2,0:T(8,128)S(1)} all-to-all(f32[4,1024,256]{1,2,0:T(8,128)S(1)} %bitcast.64), channel_id=1, replica_groups=mesh['tm'=64,'chan'=4] {'chan'}, dimensions={0} | all-to-all | bytes 8388608 | tf_op jit(solution)/shard_map/all_to_all | solution.py:41
  120.4 14.9 %fusion.48 = f32[1024,1024]{0,1:T(8,128)} fusion(f32[1024,1024]{0,1:T(8,128)S(1)} %bitcast.66), kind=kOutput, calls=%fused_computation.117 | convolution fusion | flops 12884901888 | bytes 8388608 | tf_op jit(solution)/shard_map/dot_general | solution.py:43
  135.3 97.6 %all-reduce.4.cloned.1.call-done = f32[1024,1024]{0,1:T(8,128)} async-done(((f32[1024,1024]{0,1:T(8,128)}), f32[1024,1024]{0,1:T(8,128)}) %all-reduce.4.cloned.1.call-update) | async-done | bytes 4194320 | tf_op jit(solution)/shard_map/psum | solution.py:52
  233.0 200.2 %all-reduce.6.cloned.1.call-done = f32[1024,1024]{0,1:T(8,128)} async-done(((f32[1024,1024]{0,1:T(8,128)}), f32[1024,1024]{0,1:T(8,128)}) %all-reduce.6.cloned.1.call-update) | async-done | bytes 4194320 | tf_op jit(solution)/shard_map/psum | solution.py:52
  433.2 5.0 broadcast_multiply_fusion
  438.3 5.8 copy.9
  444.1 4.4 fusion
  450.5 11.7 %cholesky.223 = f32[128,128]{1,0:T(8,128)S(1)} custom-call(f32[128,128]{1,0:T(8,128)S(1)} %cholesky.580), custom_call_target="Cholesky" | custom-call | tf_op jit(solution)/shard_map/jit(cholesky)/cholesky | solution.py:53
  462.3 9.8 %custom-call.59 = f32[1,128,128]{1,2,0:T(8,128)S(1)} custom-call(f32[1,128,128]{2,1,0:T(8,128)S(1)} %get-tuple-element.26), custom_call_target="InvertDiagBlocksLowerTriangular" | custom-call | tf_op jit(solution)/shard_map/jit(cholesky)/cholesky | solution.py:53
  472.1 2.5 cholesky.255
  474.6 2.3 constant_dynamic-update-slice_fusion
  478.5 11.9 %cholesky.244 = f32[128,128]{1,0:T(8,128)S(1)} custom-call(f32[128,128]{1,0:T(8,128)S(1)} %cholesky.584), custom_call_target="Cholesky" | custom-call | tf_op jit(solution)/shard_map/jit(cholesky)/cholesky | solution.py:53
  491.0 9.8 %custom-call.60 = f32[1,128,128]{1,2,0:T(8,128)S(1)} custom-call(f32[1,128,128]{2,1,0:T(8,128)S(1)} %get-tuple-element.23), custom_call_target="InvertDiagBlocksLowerTriangular" | custom-call | tf_op jit(solution)/shard_map/jit(cholesky)/cholesky | solution.py:53
  502.0 2.1 convolution_subtract_fusion.1
  504.1 11.7 %cholesky.468 = f32[128,128]{1,0:T(8,128)S(1)} custom-call(f32[128,128]{1,0:T(8,128)S(1)} %cholesky.589), custom_call_target="Cholesky" | custom-call | tf_op jit(solution)/shard_map/jit(cholesky)/cholesky | solution.py:53
  517.1 9.8 %custom-call.61 = f32[1,128,128]{1,2,0:T(8,128)S(1)} custom-call(f32[1,128,128]{2,1,0:T(8,128)S(1)} %get-tuple-element.20), custom_call_target="InvertDiagBlocksLowerTriangular" | custom-call | tf_op jit(solution)/shard_map/jit(cholesky)/cholesky | solution.py:53
  528.1 2.3 convolution_subtract_fusion.2
  530.4 11.9 %cholesky.487 = f32[128,128]{1,0:T(8,128)S(1)} custom-call(f32[128,128]{1,0:T(8,128)S(1)} %cholesky.594), custom_call_target="Cholesky" | custom-call | tf_op jit(solution)/shard_map/jit(cholesky)/cholesky | solution.py:53
  543.7 9.8 %custom-call.62 = f32[1,128,128]{1,2,0:T(8,128)S(1)} custom-call(f32[1,128,128]{2,1,0:T(8,128)S(1)} %get-tuple-element.17), custom_call_target="InvertDiagBlocksLowerTriangular" | custom-call | tf_op jit(solution)/shard_map/jit(cholesky)/cholesky | solution.py:53
  554.5 2.4 convolution_subtract_fusion.3
  556.9 11.7 %cholesky.506 = f32[128,128]{1,0:T(8,128)S(1)} custom-call(f32[128,128]{1,0:T(8,128)S(1)} %cholesky.599), custom_call_target="Cholesky" | custom-call | tf_op jit(solution)/shard_map/jit(cholesky)/cholesky | solution.py:53
  570.0 10.2 %custom-call.63 = f32[1,128,128]{1,2,0:T(8,128)S(1)} custom-call(f32[1,128,128]{2,1,0:T(8,128)S(1)} %get-tuple-element.14), custom_call_target="InvertDiagBlocksLowerTriangular" | custom-call | tf_op jit(solution)/shard_map/jit(cholesky)/cholesky | solution.py:53
  581.2 2.3 convolution_subtract_fusion.4
  583.5 11.7 %cholesky.526 = f32[128,128]{1,0:T(8,128)S(1)} custom-call(f32[128,128]{1,0:T(8,128)S(1)} %cholesky.604), custom_call_target="Cholesky" | custom-call | tf_op jit(solution)/shard_map/jit(cholesky)/cholesky | solution.py:53
  596.5 9.8 %custom-call.64 = f32[1,128,128]{1,2,0:T(8,128)S(1)} custom-call(f32[1,128,128]{2,1,0:T(8,128)S(1)} %get-tuple-element.11), custom_call_target="InvertDiagBlocksLowerTriangular" | custom-call | tf_op jit(solution)/shard_map/jit(cholesky)/cholesky | solution.py:53
  609.2 11.9 %cholesky.546 = f32[128,128]{1,0:T(8,128)S(1)} custom-call(f32[128,128]{1,0:T(8,128)S(1)} %cholesky.609), custom_call_target="Cholesky" | custom-call | tf_op jit(solution)/shard_map/jit(cholesky)/cholesky | solution.py:53
  622.4 9.8 %custom-call.65 = f32[1,128,128]{1,2,0:T(8,128)S(1)} custom-call(f32[1,128,128]{2,1,0:T(8,128)S(1)} %get-tuple-element.8), custom_call_target="InvertDiagBlocksLowerTriangular" | custom-call | tf_op jit(solution)/shard_map/jit(cholesky)/cholesky | solution.py:53
  634.8 11.7 %cholesky.564 = f32[128,128]{1,0:T(8,128)S(1)} custom-call(f32[128,128]{1,0:T(8,128)S(1)} %convolution_subtract_fusion.6), custom_call_target="Cholesky" | custom-call | tf_op jit(solution)/shard_map/jit(cholesky)/cholesky | solution.py:53
  653.5 4.8 select_bitcast_fusion
  658.3 5.3 copy.10
  (55 shorter events, 29.2 us)
Async XLA Ops:
  6.5 41.7 %copy-start.1 = (s32[8]{0:T(128)S(1)}, s32[8]{0:T(128)}, u32[]{:S(2)}) copy-start(s32[8]{0:T(128)} %param.5) | copy-start | bytes 100
  6.5 39.3 %reduce-scatter.2.cloned.1.call-start = ((), (), s32[]{:S(2)}) async-start(), calls=%async_computation.2 | async-start | bytes 2621440 | tf_op jit(solution)/shard_map/reduce_scatter | solution.py:28
  11.7 221.2 %all-reduce.4.cloned.1.call-start = ((), (), s32[]{:S(2)}) async-start(), calls=%async_computation.3 | async-start | bytes 8388608 | tf_op jit(solution)/shard_map/psum | solution.py:52
  46.9 16.8 %collective-permute-start = (f32[512,32]{0,1:T(8,128)S(1)}, f32[512,32]{0,1:T(8,128)S(1)}, u32[]{:S(2)}, u32[]{:S(2)}) collective-permute-start(f32[512,32]{0,1:T(8,128)S(1)} %slice.213), channel_id=1, source_target_pairs={{4,0},{8,4},{12,8},{16,12},{20,16},{24,20},{28,24},{32,28},{36,32}... | collective-permute-start | bytes 196616 | tf_op jit(solution)/shard_map/ppermute | solution.py:15
  135.3 297.9 %all-reduce.6.cloned.1.call-start = ((), (), s32[]{:S(2)}) async-start(), calls=%async_computation.4 | async-start | bytes 8388608 | tf_op jit(solution)/shard_map/psum | solution.py:52
  448.6 1.9 copy-start
Sparse Core Ops, SparseCore 0:
  11.9 33.9 reduce-scatter.1
  135.4 97.4 all-reduce.3
  236.5 196.6 all-reduce.5
